TPU v7x, 512 devices: a whole 4x4x16 slice. The times are simulated.
512 devices in a mesh: ctx: 64 (over z_lo, y, core), head: 8 (over z_hi, x).
Axes of the slice: x: 4, y: 4, z: 16 (z_hi: 2, z_lo: 8; z = z_hi * 8 + z_lo), core: 2. Of those that a mesh axis runs over, the one named last changes fastest.
Arguments:
- queries: bfloat16 [8192, 4096], P('ctx', 'head'), may hold values from -8 to 8
- keys: bfloat16 [8192, 1024], P('ctx', 'head'), may hold values from -6 to 6
- values: bfloat16 [8192, 1024], P('ctx', 'head'), may hold values from -6 to 6
- out_weight: bfloat16 [4096, 8192], P('head', 'ctx'), may hold values from -2.390625 to 2.390625
- block_order: int32 [128], replicated, may hold values from 0 to 127, as said below
Outputs:
- projected: bfloat16 [8192, 8192], P('ctx', 'head')
Inputs may be any that keep to these rules, and one draw needn't show every extreme that they name: `block_order`: slot blocks 2 s and 2 s + 1 hold the position blocks p and 127 - p for some p, and each position block is held by exactly one slot block.
All inputs are finite; a program needn't handle non-finite values.
Results may differ from a plain program's by a relative error of at most 0.018.
Values may be sent and summed in bfloat16 or wider, within the bound.
No kernel may reach another device: no remote copies, remote signals or barrier semaphores. Data moves between devices by JAX's collectives and lax.ppermute only.
A program may use at most 128 MiB of HBM per device.

v0:
```python
import math
import jax
import jax.numpy as jnp
from jax import lax
from jax.sharding import PartitionSpec as P


def slot_positions(block_order, offset, number, block_len):
    row_index = offset + jnp.arange(number, dtype=jnp.int32)
    which_block = row_index // block_len
    matches = which_block[:, None] == jnp.arange(block_order.shape[0], dtype=jnp.int32)[None, :]
    block_start = jnp.sum(jnp.where(matches, block_order[None, :], 0), axis=1)
    return block_start * block_len + row_index % block_len


def local(queries, keys, values, out_weight, block_order):
    tok_rows = queries.shape[0]
    head_size = keys.shape[1]
    local_heads = queries.shape[1] // head_size
    block_len = tok_rows // 2
    query_heads = queries.reshape(tok_rows, local_heads, head_size)
    query_pos = slot_positions(block_order, lax.axis_index("ctx") * tok_rows, tok_rows, block_len)
    scaling = 1.0 / math.sqrt(head_size)
    running_max = jnp.full((local_heads, tok_rows), -1e30, jnp.float32)
    key_piece = lax.all_gather(keys, "ctx", axis=0, tiled=True)
    value_piece = lax.all_gather(values, "ctx", axis=0, tiled=True)
    key_pos = slot_positions(block_order, jnp.int32(0), key_piece.shape[0], block_len)
    scores = (
        jnp.einsum("thd,sd->hts", query_heads, key_piece, preferred_element_type=jnp.float32)
        * scaling
    )
    visible = key_pos[None, None, :] <= query_pos[None, :, None]
    scores = jnp.where(visible, scores, -1e30)
    new_max = jnp.maximum(running_max, jnp.max(scores, axis=-1))
    weights_now = jnp.where(visible, jnp.exp(scores - new_max[..., None]), 0.0)
    new_sum = jnp.sum(weights_now, axis=-1)
    weights_b = weights_now.astype(jnp.bfloat16)
    new_accum = jnp.einsum(
        "hts,sd->htd", weights_b, value_piece, preferred_element_type=jnp.float32
    )
    attended = (new_accum / new_sum[..., None]).astype(jnp.bfloat16)
    piece = lax.all_gather(out_weight, "ctx", axis=1, tiled=True)
    weight_heads = piece.reshape(local_heads, head_size, piece.shape[1])
    partial_value = jnp.einsum(
        "htd,hdc->htc", attended, weight_heads, preferred_element_type=jnp.float32
    ).astype(jnp.bfloat16)
    partial_value = lax.optimization_barrier(partial_value)
    term = jnp.sum(partial_value.astype(jnp.float32), axis=0)
    summed = lax.psum_scatter(term.astype(jnp.bfloat16), "head", scatter_dimension=1, tiled=True)
    return summed


def solution(mesh):
    in_specs = (P("ctx", "head"), P("ctx", "head"), P("ctx", "head"), P("head", "ctx"), P())
    out_specs = P("ctx", "head")
    return jax.shard_map(local, mesh=mesh, in_specs=in_specs, out_specs=out_specs, check_vma=False)
```

profile of v0, /device:TPU:8, one launch (start us, length us, event | category | flops | bytes accessed | tf_op | source)
XLA Modules:
  0.0 563.2 jit_solution(5981867400463570871)
XLA Ops:
  6.5 0.0 copy-start
  6.5 0.0 all-gather.4.cloned.1.call-start
  6.5 0.7 all-gather.4.cloned.1.call-update
  7.3 0.0 all-gather.6.cloned.1.call-start
  7.3 0.7 all-gather.6.cloned.1.call-update
  8.0 0.0 all-gather.8.cloned.1.call-start
  8.1 0.7 all-gather.8.cloned.1.call-update
  8.7 0.0 reduce-scatter.2.cloned.1.call-start
  8.8 0.8 select_reduce_fusion.1
  9.7 3.2 select_reduce_fusion
  12.9 3.7 broadcast_compare_fusion
  16.6 117.2 %all-gather.4.cloned.1.call-done = bf16[8192,128]{1,0:T(8,128)(2,1)} async-done(((bf16[128,128]{1,0:T(8,128)(2,1)}), bf16[8192,128]{1,0:T(8,128)(2,1)}) %all-gather.4.cloned.1.call-update) | async-done | bytes 2097168 | tf_op jit(solution)/shard_map/all_gather | solution.py:25
  133.8 0.0 copy-done
  133.8 3.8 fusion
  137.6 0.0 copy-start.1
  137.6 5.7 %copy-done.1 = f32[8192,128,4]{1,0,2:T(8,128)} copy-done((f32[8192,128,4]{1,0,2:T(8,128)}, f32[8192,128,4]{1,0,2:T(8,128)S(1)}, u32[]{:S(2)}) %copy-start.1) | copy-done | bytes 16777240
  143.3 4.2 fusion.1
  147.5 105.0 %all-gather.6.cloned.1.call-done = bf16[8192,128]{1,0:T(8,128)(2,1)} async-done(((bf16[128,128]{1,0:T(8,128)(2,1)}), bf16[8192,128]{1,0:T(8,128)(2,1)}) %all-gather.6.cloned.1.call-update) | async-done | bytes 2097168 | tf_op jit(solution)/shard_map/all_gather | solution.py:26
  252.5 137.7 %all-gather.8.cloned.1.call-done = bf16[512,8192]{1,0:T(8,128)(2,1)} async-done(((bf16[512,128]{1,0:T(8,128)(2,1)}), bf16[512,8192]{1,0:T(8,128)(2,1)}) %all-gather.8.cloned.1.call-update) | async-done | bytes 8388624 | tf_op jit(solution)/shard_map/all_gather | solution.py:42
  390.3 15.4 %convolution_convert_fusion = bf16[4,128,8192]{2,1,0:T(8,128)(2,1)} fusion(bf16[4,128,8192]{2,1,0:T(8,128)(2,1)} %bitcast.42, bf16[8192,128]{1,0:T(8,128)(2,1)} %all-gather.6.cloned.1.call-done, f32[8192,128,4]{1,0,2:T(8,128)} %copy-done.1, f32[4,128]{1,0:T(4,128)S(1)} %broadcast_maximum_fusion, pred[128,8192]{0,1:T(8,128)(4,1)S(1)} %broadcast_compare_fusion, ...), kind=kOutput, calls=%fused_computation.3 | convolution fusion | flops 2172780544 | bytes 36704256 | tf_op jit(solution)/shard_map/htd,hdc->htc/dot_general | solution.py:44
  405.7 6.9 %reduce_sum.42 = bf16[128,8192]{1,0:T(8,128)(2,1)} reduce(bf16[4,128,8192]{2,1,0:T(8,128)(2,1)} %convolution_convert_fusion, bf16[]{:T(256)} %constant.69.clone.1), dimensions={0}, to_apply=%region_4.5 | reduce | flops 3145728 | bytes 10485762 | tf_op jit(solution)/shard_map/reduce_sum | solution.py:48
  412.6 0.0 reduce-scatter.2.cloned.1.call-update
  412.6 144.0 %reduce-scatter.2.cloned.1.call-done = bf16[128,1024]{1,0:T(8,128)(2,1)} async-done(((bf16[128,8192]{1,0:T(8,128)(2,1)}), bf16[128,1024]{1,0:T(8,128)(2,1)}) %reduce-scatter.2.cloned.1.call-update) | async-done | bytes 262160 | tf_op jit(solution)/shard_map/reduce_scatter | solution.py:49
  (5 shorter events, 0.0 us)
Async XLA Ops:
  6.5 127.3 %copy-start = (bf16[128,512]{1,0:T(8,128)(2,1)S(1)}, bf16[128,512]{1,0:T(8,128)(2,1)}, u32[]{:S(2)}) copy-start(bf16[128,512]{1,0:T(8,128)(2,1)} %param.5) | copy-start | bytes 393220
  6.5 127.3 %all-gather.4.cloned.1.call-start = ((), (), s32[]{:S(2)}) async-start(), calls=%async_computation.1 | async-start | bytes 2129920 | tf_op jit(solution)/shard_map/all_gather | solution.py:25
  7.3 245.3 %all-gather.6.cloned.1.call-start = ((), (), s32[]{:S(2)}) async-start(), calls=%async_computation.2 | async-start | bytes 2129920 | tf_op jit(solution)/shard_map/all_gather | solution.py:26
  8.0 382.3 %all-gather.8.cloned.1.call-start = ((), (), s32[]{:S(2)}) async-start(), calls=%async_computation.3 | async-start | bytes 8519680 | tf_op jit(solution)/shard_map/all_gather | solution.py:42
  8.7 547.9 %reduce-scatter.2.cloned.1.call-start = ((), (), s32[]{:S(2)}) async-start(), calls=%async_computation.4 | async-start | bytes 2359296 | tf_op jit(solution)/shard_map/reduce_scatter | solution.py:49
  137.6 5.7 %copy-start.1 = (f32[8192,128,4]{1,0,2:T(8,128)}, f32[8192,128,4]{1,0,2:T(8,128)S(1)}, u32[]{:S(2)}) copy-start(f32[8192,128,4]{1,0,2:T(8,128)S(1)} %get-tuple-element.6) | copy-start | bytes 50331652
Sparse Core Ops, SparseCore 0:
  9.5 124.2 all-gather.3
  136.0 116.4 all-gather.5
  254.6 135.6 all-gather.7
  412.7 143.8 reduce-scatter.1
where the time goes:
time: 563 us
  waiting for transfers between devices  506 us (90%)
  matrix products  19.2 us (3%)
  other arithmetic  18.8 us (3%)
  between operations  13.2 us (2%)
  local copies, waits for them, and re-layouts  5.7 us (1%)
    reduce_scatter x1, waiting for transfers between devices, local(): lax.psum_scatter(term.astype(jnp.bfloat16), 'head', scatter_dimension=1,...  144 us
    all_gather x1, waiting for transfers between devices, local(): piece = lax.all_gather(out_weight, 'ctx', axis=1, tiled=True)  138 us
    all_gather x1, waiting for transfers between devices, local(): key_piece = lax.all_gather(keys, 'ctx', axis=0, tiled=True)  117 us
    all_gather x1, waiting for transfers between devices, local(): value_piece = lax.all_gather(values, 'ctx', axis=0, tiled=True)  105 us
    dot_general x1, matrix products, local(): jnp.einsum('htd,hdc->htc', attended, weight_heads, preferred_element_type...  15.4 us
  transfers between devices with their start and end apart: 4, of which 4 were waited for; matrix products, arithmetic and copies ran while one was open for 3% of the time, Pallas kernels for 0%

commit v1 on v0

--- a/solution.py
+++ b/solution.py
@@ -23,7 +23,8 @@
     scaling = 1.0 / math.sqrt(head_size)
     running_max = jnp.full((local_heads, tok_rows), -1e30, jnp.float32)
     key_piece = lax.all_gather(keys, "ctx", axis=0, tiled=True)
-    value_piece = lax.all_gather(values, "ctx", axis=0, tiled=True)
+    sent = jnp.stack([values] * lax.axis_size("ctx"))
+    value_piece = jnp.concatenate(lax.all_to_all(sent, "ctx", 0, 0), axis=0)
     key_pos = slot_positions(block_order, jnp.int32(0), key_piece.shape[0], block_len)
     scores = (
         jnp.einsum("thd,sd->hts", query_heads, key_piece, preferred_element_type=jnp.float32)

time: 563 us -> 488 us (0.87)
  the two profiles are of different devices: /device:TPU:8 before, /device:TPU:16 now
where the time goes in v1:
time: 488 us
  waiting for transfers between devices  413 us (85%)
  other arithmetic  18.8 us (4%)
  matrix products  18.6 us (4%)
  starting transfers between devices  16.1 us (3%)
  between operations  13.2 us (3%)
  local copies, waits for them, and re-layouts  8.36 us (2%)
    reduce_scatter x1, waiting for transfers between devices, local(): lax.psum_scatter(term.astype(jnp.bfloat16), 'head', scatter_dimension=1,...  145 us
    all_gather x1, waiting for transfers between devices, local(): key_piece = lax.all_gather(keys, 'ctx', axis=0, tiled=True)  142 us
    all_gather x1, waiting for transfers between devices, local(): piece = lax.all_gather(out_weight, 'ctx', axis=1, tiled=True)  124 us
    all_to_all x1, starting transfers between devices, local(): value_piece = jnp.concatenate(lax.all_to_all(sent, 'ctx', 0, 0), axis=0)  16 us
    dot_general x1, matrix products, local(): jnp.einsum('htd,hdc->htc', attended, weight_heads, preferred_element_type...  14.8 us
  transfers between devices with their start and end apart: 4, of which 3 were waited for; matrix products, arithmetic and copies ran while one was open for 4% of the time, Pallas kernels for 0%

profile of v1, /device:TPU:16, one launch (start us, length us, event | category | flops | bytes accessed | tf_op | source)
XLA Modules:
  0.0 487.8 jit_solution(15463399714420570460)
XLA Ops:
  6.5 0.0 copy-start
  6.5 0.0 all-gather.3.cloned.1.call-start
  6.5 0.7 all-gather.3.cloned.1.call-update
  7.3 0.0 all-gather.5.cloned.1.call-start
  7.3 0.7 all-gather.5.cloned.1.call-update
  8.0 2.7 stack.2
  10.7 16.0 %all-to-all-start = ((bf16[64,128,128]{2,1,0:T(8,128)(2,1)}), bf16[64,128,128]{2,1,0:T(8,128)(2,1)S(1)}, u32[]{:S(2)}, u32[]{:S(2)}) async-start(bf16[64,128,128]{2,1,0:T(8,128)(2,1)} %stack.2), calls=%async_computation | async-start | bytes 4194304 | tf_op jit(solution)/shard_map/all_to_all | solution.py:27
  26.7 0.0 reduce-scatter.2.cloned.1.call-start
  26.8 0.8 select_reduce_fusion.1
  27.6 3.2 select_reduce_fusion
  30.9 3.7 broadcast_compare_fusion
  34.6 141.9 %all-gather.3.cloned.1.call-done = bf16[8192,128]{1,0:T(8,128)(2,1)} async-done(((bf16[128,128]{1,0:T(8,128)(2,1)}), bf16[8192,128]{1,0:T(8,128)(2,1)}) %all-gather.3.cloned.1.call-update) | async-done | bytes 2097168 | tf_op jit(solution)/shard_map/all_gather | solution.py:25
  176.5 0.0 copy-done
  176.5 3.8 fusion
  180.3 0.0 copy-start.1
  180.3 5.7 %copy-done.1 = f32[8192,128,4]{1,0,2:T(8,128)} copy-done((f32[8192,128,4]{1,0,2:T(8,128)}, f32[8192,128,4]{1,0,2:T(8,128)S(1)}, u32[]{:S(2)}) %copy-start.1) | copy-done | bytes 16777240
  186.0 4.2 fusion.1
  190.2 0.0 all-to-all-done
  190.2 124.5 %all-gather.5.cloned.1.call-done = bf16[512,8192]{1,0:T(8,128)(2,1)} async-done(((bf16[512,128]{1,0:T(8,128)(2,1)}), bf16[512,8192]{1,0:T(8,128)(2,1)}) %all-gather.5.cloned.1.call-update) | async-done | bytes 8388624 | tf_op jit(solution)/shard_map/all_gather | solution.py:43
  314.6 14.8 %convolution_convert_fusion = bf16[4,128,8192]{2,1,0:T(8,128)(2,1)} fusion(bf16[4,128,8192]{2,1,0:T(8,128)(2,1)} %bitcast.38, bf16[8192,128,1]{1,0,2:T(8,128)(2,1)S(1)} %bitcast.37, f32[8192,128,4]{1,0,2:T(8,128)} %copy-done.1, f32[4,128]{1,0:T(4,128)S(1)} %broadcast_maximum_fusion, pred[128,8192]{0,1:T(8,128)(4,1)S(1)} %broadcast_compare_fusion, ...), kind=kOutput, calls=%fused_computation.3 | convolution fusion | flops 2172780544 | bytes 36704256 | tf_op jit(solution)/shard_map/htd,hdc->htc/dot_general | solution.py:45
  329.5 6.9 %reduce_sum.42 = bf16[128,8192]{1,0:T(8,128)(2,1)} reduce(bf16[4,128,8192]{2,1,0:T(8,128)(2,1)} %convolution_convert_fusion, bf16[]{:T(256)} %constant.69.clone.1), dimensions={0}, to_apply=%region_4.5 | reduce | flops 3145728 | bytes 10485762 | tf_op jit(solution)/shard_map/reduce_sum | solution.py:49
  336.4 0.0 reduce-scatter.2.cloned.1.call-update
  336.4 144.9 %reduce-scatter.2.cloned.1.call-done = bf16[128,1024]{1,0:T(8,128)(2,1)} async-done(((bf16[128,8192]{1,0:T(8,128)(2,1)}), bf16[128,1024]{1,0:T(8,128)(2,1)}) %reduce-scatter.2.cloned.1.call-update) | async-done | bytes 262160 | tf_op jit(solution)/shard_map/reduce_scatter | solution.py:50
  (5 shorter events, 0.0 us)
Async XLA Ops:
  6.5 170.0 %copy-start = (bf16[128,512]{1,0:T(8,128)(2,1)S(1)}, bf16[128,512]{1,0:T(8,128)(2,1)}, u32[]{:S(2)}) copy-start(bf16[128,512]{1,0:T(8,128)(2,1)} %param.5) | copy-start | bytes 393220
  6.5 170.0 %all-gather.3.cloned.1.call-start = ((), (), s32[]{:S(2)}) async-start(), calls=%async_computation.2 | async-start | bytes 2129920 | tf_op jit(solution)/shard_map/all_gather | solution.py:25
  7.3 307.4 %all-gather.5.cloned.1.call-start = ((), (), s32[]{:S(2)}) async-start(), calls=%async_computation.3 | async-start | bytes 8519680 | tf_op jit(solution)/shard_map/all_gather | solution.py:43
  10.7 179.5 %all-to-all-start = ((bf16[64,128,128]{2,1,0:T(8,128)(2,1)}), bf16[64,128,128]{2,1,0:T(8,128)(2,1)S(1)}, u32[]{:S(2)}, u32[]{:S(2)}) async-start(bf16[64,128,128]{2,1,0:T(8,128)(2,1)} %stack.2), calls=%async_computation | async-start | bytes 4194304 | tf_op jit(solution)/shard_map/all_to_all | solution.py:27
  26.7 454.6 %reduce-scatter.2.cloned.1.call-start = ((), (), s32[]{:S(2)}) async-start(), calls=%async_computation.4 | async-start | bytes 2359296 | tf_op jit(solution)/shard_map/reduce_scatter | solution.py:50
  180.3 5.7 %copy-start.1 = (f32[8192,128,4]{1,0,2:T(8,128)}, f32[8192,128,4]{1,0,2:T(8,128)S(1)}, u32[]{:S(2)}) copy-start(f32[8192,128,4]{1,0,2:T(8,128)S(1)} %get-tuple-element.6) | copy-start | bytes 50331652
Sparse Core Ops, SparseCore 0:
  9.5 166.9 all-gather.2
  178.6 136.0 all-gather.4
  336.5 144.7 reduce-scatter.1
